TPU v7x, 32 devices: a whole 2x2x4 slice. The times are simulated.
32 devices in a mesh: hid: 4 (over y, x), tok: 8 (over z, core).
Axes of the slice: x: 2, y: 2, z: 4, core: 2. Of those that a mesh axis runs over, the one named last changes fastest.
Arguments:
- keys: bfloat16 [2, 512, 1280], P(None, 'tok'), may hold values from -6 to 6
- values: bfloat16 [2, 512, 1280], P(None, 'tok'), may hold values from -6 to 6
- queries: bfloat16 [512, 1280], P('tok'), may hold values from -6 to 6
- rates: float32 [2, 512], P(None, 'tok'), may hold values from 0.01 to 0.1
- forget: float32 [2], replicated, may hold values from 0.05 to 0.3
- momentum: float32 [1], replicated, may hold values from 0.5 to 0.95
- write_weight: float32 [1280, 1280], P('tok', 'hid'), may hold values from -0.15625 to 0.15625
- read_weight: float32 [1280, 1280], P('tok', 'hid'), may hold values from -0.15625 to 0.15625
Outputs:
- new_write: float32 [1280, 1280], P('tok', 'hid')
- new_read: float32 [1280, 1280], P('tok', 'hid')
- recalled: bfloat16 [512, 1280], P('tok')
All inputs are finite; a program needn't handle non-finite values.
Results may differ from a plain program's by a relative error of at most 0.003.
Values may be sent and summed in bfloat16 or wider, within the bound.
No kernel may reach another device: no remote copies, remote signals or barrier semaphores. Data moves between devices by JAX's collectives and lax.ppermute only.
A program may use at most 64 MiB of HBM per device.

v0:
```python
import jax
import jax.numpy as jnp
from jax import lax
from jax.sharding import PartitionSpec as P

highest = lax.Precision.HIGHEST
radius = 12.0


def silu_slope(z):
    sig = jax.nn.sigmoid(z)
    return sig * (1.0 + z * (1.0 - sig))


def times_transposed(left, right):
    return lax.dot_general(left, right, (((1,), (1,)), ((), ())), precision=highest)


def inner_rows(left, right):
    return lax.dot_general(left, right, (((0,), (0,)), ((), ())), precision=highest)


def on_device(keys, values, queries, rates, forget, momentum, write_weight, read_weight):
    width = keys.shape[2]
    full_write, full_read = (
        lax.all_gather(write_weight, "tok", axis=0, tiled=True),
        lax.all_gather(read_weight, "tok", axis=0, tiled=True),
    )
    inputs = keys.reshape(-1, width).astype(jnp.float32)
    hidden_pre = jnp.dot(inputs, full_write, precision=highest)
    hidden = jax.nn.silu(hidden_pre)
    output = lax.psum(times_transposed(hidden, full_read).astype(jnp.bfloat16), "hid").astype(
        jnp.float32
    )
    error = inputs + output - values.reshape(-1, width).astype(jnp.float32)
    factor = 1.0 - forget[1] + momentum[0]
    per_block = jnp.stack([factor, jnp.ones_like(factor)])
    row_scale = (2.0 * rates * per_block[:, None]).reshape(-1, 1)
    delta = row_scale * error
    back = jnp.dot(delta, full_read, precision=highest) * silu_slope(hidden_pre)
    grad_write = inner_rows(inputs, back)
    grad_read = inner_rows(delta, hidden)
    part_w, part_r = (
        lax.psum_scatter(grad_write, "tok", scatter_dimension=0, tiled=True),
        lax.psum_scatter(grad_read, "tok", scatter_dimension=0, tiled=True),
    )
    keep = (1.0 - forget[0]) * (1.0 - forget[1])
    whole_w, whole_r = (
        lax.all_gather(part_w, "tok", axis=0, tiled=True),
        lax.all_gather(part_r, "tok", axis=0, tiled=True),
    )
    total = lax.psum(jnp.sum(whole_w * whole_w) + jnp.sum(whole_r * whole_r), "hid")
    scale = jnp.minimum(1.0, radius / jnp.sqrt(total + 1e-06))
    new_write = keep * write_weight - scale * part_w
    new_read = keep * read_weight - scale * part_r
    wide_write = keep * full_write - scale * whole_w
    wide_read = keep * full_read - scale * whole_r
    asked = queries.astype(jnp.float32)
    query_hidden = jax.nn.silu(jnp.dot(asked, wide_write, precision=highest))
    answer = lax.psum(times_transposed(query_hidden, wide_read), "hid")
    recalled = (asked + answer).astype(jnp.bfloat16)
    return (new_write, new_read, recalled)


def solution(mesh):
    in_specs = (
        P(None, "tok", None),
        P(None, "tok", None),
        P("tok", None),
        P(None, "tok"),
        P(),
        P(),
        P("tok", "hid"),
        P("tok", "hid"),
    )
    out_specs = (P("tok", "hid"), P("tok", "hid"), P("tok", None))
    return jax.shard_map(
        on_device, mesh=mesh, in_specs=in_specs, out_specs=out_specs, check_vma=False
    )
```

profile of v0, /device:TPU:0, one launch (start us, length us, event | category | flops | bytes accessed | tf_op | source)
XLA Modules:
  0.0 327.0 jit_solution(6038212173051882562)
XLA Ops:
  7.2 0.0 all-gather.5.cloned.1.call-start
  7.2 0.7 all-gather.5.cloned.1.call-update
  7.9 0.0 all-gather.7.cloned.1.call-start
  7.9 0.7 all-gather.7.cloned.1.call-update
  8.6 0.0 all-reduce.3.cloned.1.call-start
  9.3 1.3 fusion.33
  11.3 29.1 %all-gather.5.cloned.1.call-done = f32[1280,320]{1,0:T(8,128)} async-done(((f32[160,320]{1,0:T(8,128)}), f32[1280,320]{1,0:T(8,128)}) %all-gather.5.cloned.1.call-update) | async-done | bytes 1638416 | tf_op jit(solution)/shard_map/all_gather | solution.py:26
  40.4 3.4 %fusion.34 = f32[128,320]{0,1:T(8,128)S(1)} fusion(bf16[128,1280]{1,0:T(8,128)(2,1)} %bitcast.17, f32[1280,320]{1,0:T(8,128)} %all-gather.5.cloned.1.call-done), kind=kOutput, calls=%fused_computation.40 | convolution fusion | flops 629145600 | bytes 2129920 | tf_op jit(solution)/shard_map/dot_general | solution.py:30
  43.8 0.0 copy-start.10
  43.8 0.0 copy-start.2
  43.8 0.0 copy-start.3
  43.8 25.7 %all-gather.7.cloned.1.call-done = f32[1280,320]{1,0:T(8,128)} async-done(((f32[160,320]{1,0:T(8,128)}), f32[1280,320]{1,0:T(8,128)}) %all-gather.7.cloned.1.call-update) | async-done | bytes 1638416 | tf_op jit(solution)/shard_map/all_gather | solution.py:27
  69.6 4.6 %convolution_convert_fusion = bf16[128,1280]{1,0:T(8,128)(2,1)} fusion(f32[1280,320]{1,0:T(8,128)} %all-gather.7.cloned.1.call-done, f32[128,320]{0,1:T(8,128)S(1)} %fusion.34), kind=kOutput, calls=%fused_computation.1 | convolution fusion | flops 629473280 | bytes 2129920 | tf_op jit(solution)/shard_map/dot_general | solution.py:16
  74.2 0.0 all-reduce.3.cloned.1.call-update
  74.2 0.0 reduce-scatter.7.cloned.1.call-start
  74.3 0.1 maximum_multiply_fusion
  74.3 0.0 copy-done.10
  74.3 0.1 broadcast_multiply_fusion
  74.4 0.1 mul.101
  74.5 42.8 %all-reduce.3.cloned.1.call-done = bf16[128,1280]{1,0:T(8,128)(2,1)} async-done(((bf16[128,1280]{1,0:T(8,128)(2,1)}), bf16[128,1280]{1,0:T(8,128)(2,1)}) %all-reduce.3.cloned.1.call-update) | async-done | bytes 327696 | tf_op jit(solution)/shard_map/psum | solution.py:32
  117.3 0.0 copy-done.2
  117.4 0.0 copy-done.3
  117.4 0.0 copy-done
  117.4 4.3 %convolution_multiply_fusion = f32[128,320]{0,1:T(8,128)S(1)} fusion(f32[1280,320]{1,0:T(8,128)S(1)} %copy-done, bf16[128,1280]{1,0:T(8,128)(2,1)S(1)} %bitcast.21, bf16[128,1280]{1,0:T(8,128)(2,1)} %all-reduce.3.cloned.1.call-done, bf16[128,1280]{1,0:T(8,128)(2,1)S(1)} %bitcast.18, f32[128]{0:T(128)S(1)} %mul.101, f32[128,320]{0,1:T(8,128)S(1)} %fusion.34), kind=kOutput, calls=%fused_computation.12 | convolution fusion | flops 630456320 | bytes 2949632 | tf_op jit(solution)/shard_map/dot_general | solution.py:40
  121.6 2.0 convolution_bitcast_fusion
  123.6 2.8 copy.26
  126.4 0.0 reduce-scatter.7.cloned.1.call-update
  126.5 0.0 reduce-scatter.9.cloned.1.call-start
  126.5 0.0 copy-done.4
  126.5 3.7 %fusion.16 = f32[1280,320]{1,0:T(8,128)} fusion(bf16[128,1280]{1,0:T(8,128)(2,1)S(1)} %bitcast.22, bf16[128,1280]{1,0:T(8,128)(2,1)S(1)} %copy-done.4, bf16[128,1280]{1,0:T(8,128)(2,1)S(1)} %bitcast.20, f32[128]{0:T(128)S(1)} %mul.101, f32[128,320]{0,1:T(8,128)S(1)} %fusion.34), kind=kOutput, calls=%fused_computation.20 | convolution fusion | flops 630292480 | bytes 2785792
  130.2 0.0 reduce-scatter.9.cloned.1.call-update
  130.2 0.0 all-gather.9.cloned.1.call-start
  130.3 32.2 %reduce-scatter.7.cloned.1.call-done = f32[160,320]{1,0:T(8,128)} async-done(((f32[1280,320]{1,0:T(8,128)}), f32[160,320]{1,0:T(8,128)}) %reduce-scatter.7.cloned.1.call-update) | async-done | bytes 204816 | tf_op jit(solution)/shard_map/reduce_scatter | solution.py:44
  162.5 0.0 all-gather.9.cloned.1.call-update
  162.5 0.0 all-gather.11.cloned.1.call-start
  162.5 36.2 %reduce-scatter.9.cloned.1.call-done = f32[160,320]{1,0:T(8,128)} async-done(((f32[1280,320]{1,0:T(8,128)}), f32[160,320]{1,0:T(8,128)}) %reduce-scatter.9.cloned.1.call-update) | async-done | bytes 204816 | tf_op jit(solution)/shard_map/reduce_scatter | solution.py:45
  198.8 0.0 all-gather.11.cloned.1.call-update
  198.8 0.0 all-reduce.5.cloned.1.call-start
  199.5 0.0 copy-start.9
  199.5 27.1 %all-gather.9.cloned.1.call-done = f32[1280,320]{1,0:T(8,128)} async-done(((f32[160,320]{1,0:T(8,128)}), f32[1280,320]{1,0:T(8,128)}) %all-gather.9.cloned.1.call-update) | async-done | bytes 1638416 | tf_op jit(solution)/shard_map/all_gather | solution.py:49
  226.6 2.7 multiply_reduce_fusion.1
  229.3 26.5 %all-gather.11.cloned.1.call-done = f32[1280,320]{1,0:T(8,128)} async-done(((f32[160,320]{1,0:T(8,128)}), f32[1280,320]{1,0:T(8,128)}) %all-gather.11.cloned.1.call-update) | async-done | bytes 1638416 | tf_op jit(solution)/shard_map/all_gather | solution.py:50
  255.7 2.7 multiply_reduce_fusion
  259.7 10.5 %psum.22 = f32[]{:T(128)} all-reduce(f32[]{:T(128)S(6)} %add.42), channel_id=1, replica_groups=mesh['hid'=4,'tok'=8] {'hid'}, use_global_device_ids=true, to_apply=%region_5.6 | all-reduce | flops 1 | bytes 8 | tf_op jit(solution)/shard_map/psum | solution.py:52
  270.9 0.0 copy-done.9
  270.9 0.0 copy-start.1
  270.9 3.3 %fusion.8 = f32[64,320]{1,0:T(8,128)S(1)} fusion(bf16[64,1280]{1,0:T(8,128)(2,1)S(1)} %copy-done.9, f32[1280,320]{1,0:T(8,128)} %all-gather.9.cloned.1.call-done, f32[1280,320]{1,0:T(8,128)} %all-gather.5.cloned.1.call-done, f32[]{:T(128)S(6)} %min.3, f32[]{:T(128)} %bitcast), kind=kOutput, calls=%fused_computation.13 | convolution fusion | flops 315801600 | bytes 3522568 | tf_op jit(solution)/shard_map/dot_general | solution.py:59
  274.2 0.0 copy-done.1
  274.2 0.0 copy-start.5
  274.3 0.0 copy-start.6
  274.3 0.0 copy-start.7
  274.3 2.9 fusion
  277.2 0.0 all-reduce.5.cloned.1.call-update
  277.2 0.0 copy-done.5
  277.2 0.1 copy.18
  277.4 0.1 copy.22
  277.5 0.1 copy.27
  277.7 0.4 copy-done.8
  278.1 0.1 copy.29
  278.3 0.1 multiply_subtract_fusion
  278.4 0.8 copy.23
  279.2 0.8 copy.24
  280.0 38.5 %all-reduce.5.cloned.1.call-done = f32[64,1280]{1,0:T(8,128)} async-done(((f32[64,1280]{1,0:T(8,128)}), f32[64,1280]{1,0:T(8,128)}) %all-reduce.5.cloned.1.call-update) | async-done | bytes 327696 | tf_op jit(solution)/shard_map/psum | solution.py:60
  318.5 1.7 add_convert_fusion
  (5 shorter events, 0.0 us)
Async XLA Ops:
  7.2 33.3 %all-gather.5.cloned.1.call-start = ((), (), s32[]{:S(2)}) async-start(), calls=%async_computation.2 | async-start | bytes 2211840 | tf_op jit(solution)/shard_map/all_gather | solution.py:26
  7.9 61.7 %all-gather.7.cloned.1.call-start = ((), (), s32[]{:S(2)}) async-start(), calls=%async_computation.3 | async-start | bytes 2211840 | tf_op jit(solution)/shard_map/all_gather | solution.py:27
  8.6 108.7 %all-reduce.3.cloned.1.call-start = ((), (), s32[]{:S(2)}) async-start(), calls=%async_computation.4 | async-start | bytes 655360 | tf_op jit(solution)/shard_map/psum | solution.py:32
  43.8 30.5 %copy-start.10 = (f32[2,64]{1,0:T(2,128)S(1)}, f32[2,64]{1,0:T(2,128)}, u32[]{:S(2)}) copy-start(f32[2,64]{1,0:T(2,128)} %param.11) | copy-start | bytes 1540
  43.8 73.5 %copy-start.2 = (bf16[2,64,1280]{2,1,0:T(8,128)(2,1)S(1)}, bf16[2,64,1280]{2,1,0:T(8,128)(2,1)}, u32[]{:S(2)}) copy-start(bf16[2,64,1280]{2,1,0:T(8,128)(2,1)} %param.8) | copy-start | bytes 983044
  43.8 73.5 %copy-start.3 = (bf16[2,64,1280]{2,1,0:T(8,128)(2,1)S(1)}, bf16[2,64,1280]{2,1,0:T(8,128)(2,1)}, u32[]{:S(2)}) copy-start(bf16[2,64,1280]{2,1,0:T(8,128)(2,1)} %param.9) | copy-start | bytes 983044
  69.6 47.8 %copy-start = (f32[1280,320]{1,0:T(8,128)S(1)}, f32[1280,320]{1,0:T(8,128)}, u32[]{:S(2)}) copy-start(f32[1280,320]{1,0:T(8,128)} %all-gather.7.cloned.1.call-done) | copy-start | bytes 4915204
  74.2 88.2 %reduce-scatter.7.cloned.1.call-start = ((), (), s32[]{:S(2)}) async-start(), calls=%async_computation.8 | async-start | bytes 2211840 | tf_op jit(solution)/shard_map/reduce_scatter | solution.py:44
  123.6 2.9 copy-start.4
  126.5 72.3 %reduce-scatter.9.cloned.1.call-start = ((), (), s32[]{:S(2)}) async-start(), calls=%async_computation.9 | async-start | bytes 2211840 | tf_op jit(solution)/shard_map/reduce_scatter | solution.py:45
  130.2 96.4 %all-gather.9.cloned.1.call-start = ((), (), s32[]{:S(2)}) async-start(), calls=%async_computation.5 | async-start | bytes 2211840 | tf_op jit(solution)/shard_map/all_gather | solution.py:49
  162.5 93.3 %all-gather.11.cloned.1.call-start = ((), (), s32[]{:S(2)}) async-start(), calls=%async_computation.6 | async-start | bytes 2211840 | tf_op jit(solution)/shard_map/all_gather | solution.py:50
  198.8 119.7 %all-reduce.5.cloned.1.call-start = ((), (), s32[]{:S(2)}) async-start(), calls=%async_computation.7 | async-start | bytes 655360 | tf_op jit(solution)/shard_map/psum | solution.py:60
  199.5 71.5 %copy-start.9 = (bf16[64,1280]{1,0:T(8,128)(2,1)S(1)}, bf16[64,1280]{1,0:T(8,128)(2,1)}, u32[]{:S(2)}) copy-start(bf16[64,1280]{1,0:T(8,128)(2,1)} %param.10) | copy-start | bytes 491524
  270.9 3.3 %copy-start.1 = (f32[1280,320]{1,0:T(8,128)S(1)}, f32[1280,320]{1,0:T(8,128)}, u32[]{:S(2)}) copy-start(f32[1280,320]{1,0:T(8,128)} %all-gather.11.cloned.1.call-done) | copy-start | bytes 4915204
  274.2 2.9 copy-start.5
  274.3 3.1 copy-start.6
  274.3 3.2 copy-start.7
  277.2 0.9 copy-start.8
Sparse Core Ops, SparseCore 0:
  9.6 30.7 all-gather.4
  42.1 27.4 all-gather.6
  74.3 42.9 all-reduce.2
  126.6 35.8 reduce-scatter.6
  164.6 34.0 reduce-scatter.8
  200.2 26.3 all-gather.8
  228.2 27.4 all-gather.10
  277.3 41.1 all-reduce.4
where the time goes:
time: 327 us
  waiting for transfers between devices  260 us (80%)
  matrix products  24 us (7%)
  between operations  18.3 us (6%)
  blocking collectives  10.5 us (3%)
  other arithmetic  7.21 us (2%)
  local copies, waits for them, and re-layouts  6.97 us (2%)
    psum x1, waiting for transfers between devices, on_device(): lax.psum(times_transposed(hidden, full_read).astype(jnp.bfloat16), 'hid')  42.8 us
    psum x1, waiting for transfers between devices, on_device(): answer = lax.psum(times_transposed(query_hidden, wide_read), 'hid')  38.5 us
    reduce_scatter x1, waiting for transfers between devices, on_device(): lax.psum_scatter(grad_read, 'tok', scatter_dimension=0, tiled=True)  36.2 us
    reduce_scatter x1, waiting for transfers between devices, on_device(): lax.psum_scatter(grad_write, 'tok', scatter_dimension=0, tiled=True)  32.2 us
    all_gather x1, waiting for transfers between devices, on_device(): lax.all_gather(write_weight, 'tok', axis=0, tiled=True)  29.1 us
    all_gather x1, waiting for transfers between devices, on_device(): lax.all_gather(part_w, 'tok', axis=0, tiled=True)  27.1 us
    all_gather x1, waiting for transfers between devices, on_device(): lax.all_gather(part_r, 'tok', axis=0, tiled=True)  26.5 us
    all_gather x1, waiting for transfers between devices, on_device(): lax.all_gather(read_weight, 'tok', axis=0, tiled=True)  25.7 us
  transfers between devices with their start and end apart: 8, of which 8 were waited for; matrix products, arithmetic and copies ran while one was open for 4% of the time, Pallas kernels for 0%

commit v1 on v0

--- a/solution.py
+++ b/solution.py
@@ -5,6 +5,7 @@
 
 highest = lax.Precision.HIGHEST
 radius = 12.0
+draw_the_masks = lambda in_array, named_axis: jnp.sum(lax.all_gather(in_array, named_axis), 0)
 
 
 def silu_slope(z):
@@ -29,7 +30,7 @@
     inputs = keys.reshape(-1, width).astype(jnp.float32)
     hidden_pre = jnp.dot(inputs, full_write, precision=highest)
     hidden = jax.nn.silu(hidden_pre)
-    output = lax.psum(times_transposed(hidden, full_read).astype(jnp.bfloat16), "hid").astype(
+    output = draw_the_masks(times_transposed(hidden, full_read).astype(jnp.bfloat16), "hid").astype(
         jnp.float32
     )
     error = inputs + output - values.reshape(-1, width).astype(jnp.float32)

time: 327 us -> 313 us (0.957)
  waiting for transfers between devices: 260 us -> 245 us
    psum x1 -> x0, waiting for transfers between devices: 42.8 us -> none  [on_device(): lax.psum(times_transposed(hidden, full_read).astype(jnp.bfloat16), 'hid')]
    all_gather x0 -> x1, waiting for transfers between devices: none -> 26.1 us  [lax.all_gather(in_array, named_axis)]
where the time goes in v1:
time: 313 us
  waiting for transfers between devices  245 us (78%)
  matrix products  23.1 us (7%)
  between operations  18.3 us (6%)
  blocking collectives  10.5 us (3%)
  other arithmetic  8.74 us (3%)
  local copies, waits for them, and re-layouts  6.19 us (2%)
    psum x1, waiting for transfers between devices, on_device(): answer = lax.psum(times_transposed(query_hidden, wide_read), 'hid')  38.5 us
    reduce_scatter x1, waiting for transfers between devices, on_device(): lax.psum_scatter(grad_read, 'tok', scatter_dimension=0, tiled=True)  36.2 us
    reduce_scatter x1, waiting for transfers between devices, on_device(): lax.psum_scatter(grad_write, 'tok', scatter_dimension=0, tiled=True)  32.2 us
    all_gather x1, waiting for transfers between devices, on_device(): lax.all_gather(write_weight, 'tok', axis=0, tiled=True)  31.7 us
    all_gather x1, waiting for transfers between devices, on_device(): lax.all_gather(part_w, 'tok', axis=0, tiled=True)  27.1 us
    all_gather x1, waiting for transfers between devices, on_device(): lax.all_gather(part_r, 'tok', axis=0, tiled=True)  26.5 us
    all_gather x1, waiting for transfers between devices, lax.all_gather(in_array, named_axis)  26.1 us
    all_gather x1, waiting for transfers between devices, on_device(): lax.all_gather(read_weight, 'tok', axis=0, tiled=True)  25.7 us
  transfers between devices with their start and end apart: 8, of which 8 were waited for; matrix products, arithmetic and copies ran while one was open for 4% of the time, Pallas kernels for 0%

profile of v1, /device:TPU:0, one launch (start us, length us, event | category | flops | bytes accessed | tf_op | source)
XLA Modules:
  0.0 312.6 jit_solution(17086590941500771833)
XLA Ops:
  7.2 0.0 all-gather.7.cloned.1.call-start
  7.2 0.7 all-gather.7.cloned.1.call-update
  7.9 0.0 all-gather.9.cloned.1.call-start
  7.9 0.7 all-gather.9.cloned.1.call-update
  8.6 0.0 all-gather.15.cloned.1.call-start
  8.7 31.7 %all-gather.7.cloned.1.call-done = f32[1280,320]{1,0:T(8,128)} async-done(((f32[160,320]{1,0:T(8,128)}), f32[1280,320]{1,0:T(8,128)}) %all-gather.7.cloned.1.call-update) | async-done | bytes 1638416 | tf_op jit(solution)/shard_map/all_gather | solution.py:27
  40.4 3.4 %fusion.34 = f32[128,320]{0,1:T(8,128)S(1)} fusion(bf16[128,1280]{1,0:T(8,128)(2,1)} %bitcast.18, f32[1280,320]{1,0:T(8,128)} %all-gather.7.cloned.1.call-done), kind=kOutput, calls=%fused_computation.40 | convolution fusion | flops 629145600 | bytes 2129920 | tf_op jit(solution)/shard_map/dot_general | solution.py:31
  43.8 0.0 copy-start.9
  43.8 0.0 copy-start.10
  43.8 0.0 copy-start.2
  43.8 0.0 copy-start.3
  43.9 25.7 %all-gather.9.cloned.1.call-done = f32[1280,320]{1,0:T(8,128)} async-done(((f32[160,320]{1,0:T(8,128)}), f32[1280,320]{1,0:T(8,128)}) %all-gather.9.cloned.1.call-update) | async-done | bytes 1638416 | tf_op jit(solution)/shard_map/all_gather | solution.py:28
  69.6 4.6 %convolution_convert_fusion = bf16[128,1280]{1,0:T(8,128)(2,1)} fusion(f32[1280,320]{1,0:T(8,128)} %all-gather.9.cloned.1.call-done, f32[128,320]{0,1:T(8,128)S(1)} %fusion.34), kind=kOutput, calls=%fused_computation.1 | convolution fusion | flops 629473280 | bytes 2129920 | tf_op jit(solution)/shard_map/dot_general | solution.py:17
  74.2 0.0 all-gather.15.cloned.1.call-update
  74.2 0.0 reduce-scatter.7.cloned.1.call-start
  74.9 0.0 copy-done.9
  74.9 0.6 fusion.33
  76.2 0.1 maximum_multiply_fusion
  76.3 0.0 copy-done.10
  76.3 0.1 broadcast_multiply_fusion
  76.3 0.1 mul.101
  76.4 26.1 %all-gather.15.cloned.1.call-done = bf16[512,1280]{1,0:T(8,128)(2,1)} async-done(((bf16[128,1280]{1,0:T(8,128)(2,1)}), bf16[512,1280]{1,0:T(8,128)(2,1)}) %all-gather.15.cloned.1.call-update) | async-done | bytes 1310736 | tf_op jit(solution)/shard_map/all_gather | solution.py:8
  102.5 1.5 reduce_sum.30
  104.0 0.0 copy-done.2
  104.0 0.0 copy-done.3
  104.0 0.0 copy-done
  104.0 3.3 %convolution_multiply_fusion = f32[128,320]{0,1:T(8,128)S(1)} fusion(f32[1280,320]{1,0:T(8,128)S(1)} %copy-done, bf16[128,1280]{1,0:T(8,128)(2,1)S(1)} %bitcast.23, bf16[128,1280]{1,0:T(8,128)(2,1)S(1)} %reduce_sum.30, bf16[128,1280]{1,0:T(8,128)(2,1)S(1)} %bitcast.19, f32[128]{0:T(128)S(1)} %mul.101, f32[128,320]{0,1:T(8,128)S(1)} %fusion.34), kind=kOutput, calls=%fused_computation.12 | convolution fusion | flops 630456320 | bytes 2949632 | tf_op jit(solution)/shard_map/dot_general | solution.py:41
  107.3 2.0 convolution_bitcast_fusion
  109.3 2.8 copy.26
  112.1 0.0 reduce-scatter.7.cloned.1.call-update
  112.1 0.0 reduce-scatter.9.cloned.1.call-start
  112.2 3.7 %fusion.16 = f32[1280,320]{1,0:T(8,128)} fusion(bf16[128,1280]{1,0:T(8,128)(2,1)S(1)} %bitcast.24, bf16[128,1280]{1,0:T(8,128)(2,1)S(1)} %reduce_sum.30, bf16[128,1280]{1,0:T(8,128)(2,1)S(1)} %bitcast.21, f32[128]{0:T(128)S(1)} %mul.101, f32[128,320]{0,1:T(8,128)S(1)} %fusion.34), kind=kOutput, calls=%fused_computation.20 | convolution fusion | flops 630292480 | bytes 2785792
  115.8 0.0 reduce-scatter.9.cloned.1.call-update
  115.9 0.0 all-gather.11.cloned.1.call-start
  115.9 32.2 %reduce-scatter.7.cloned.1.call-done = f32[160,320]{1,0:T(8,128)} async-done(((f32[1280,320]{1,0:T(8,128)}), f32[160,320]{1,0:T(8,128)}) %reduce-scatter.7.cloned.1.call-update) | async-done | bytes 204816 | tf_op jit(solution)/shard_map/reduce_scatter | solution.py:45
  148.1 0.0 all-gather.11.cloned.1.call-update
  148.1 0.0 all-gather.13.cloned.1.call-start
  148.2 36.2 %reduce-scatter.9.cloned.1.call-done = f32[160,320]{1,0:T(8,128)} async-done(((f32[1280,320]{1,0:T(8,128)}), f32[160,320]{1,0:T(8,128)}) %reduce-scatter.9.cloned.1.call-update) | async-done | bytes 204816 | tf_op jit(solution)/shard_map/reduce_scatter | solution.py:46
  184.4 0.0 all-gather.13.cloned.1.call-update
  184.4 0.0 all-reduce.2.cloned.1.call-start
  185.1 0.0 copy-start.8
  185.1 27.1 %all-gather.11.cloned.1.call-done = f32[1280,320]{1,0:T(8,128)} async-done(((f32[160,320]{1,0:T(8,128)}), f32[1280,320]{1,0:T(8,128)}) %all-gather.11.cloned.1.call-update) | async-done | bytes 1638416 | tf_op jit(solution)/shard_map/all_gather | solution.py:50
  212.2 2.7 multiply_reduce_fusion.1
  214.8 26.5 %all-gather.13.cloned.1.call-done = f32[1280,320]{1,0:T(8,128)} async-done(((f32[160,320]{1,0:T(8,128)}), f32[1280,320]{1,0:T(8,128)}) %all-gather.13.cloned.1.call-update) | async-done | bytes 1638416 | tf_op jit(solution)/shard_map/all_gather | solution.py:51
  241.3 2.7 multiply_reduce_fusion
  245.3 10.5 %psum.14 = f32[]{:T(128)} all-reduce(f32[]{:T(128)S(6)} %add.40), channel_id=1, replica_groups=mesh['hid'=4,'tok'=8] {'hid'}, use_global_device_ids=true, to_apply=%region_5.6 | all-reduce | flops 1 | bytes 8 | tf_op jit(solution)/shard_map/psum | solution.py:53
  256.5 0.0 copy-done.8
  256.5 3.3 %fusion.8 = f32[64,320]{1,0:T(8,128)S(1)} fusion(bf16[64,1280]{1,0:T(8,128)(2,1)S(1)} %copy-done.8, f32[1280,320]{1,0:T(8,128)} %all-gather.11.cloned.1.call-done, f32[1280,320]{1,0:T(8,128)} %all-gather.7.cloned.1.call-done, f32[]{:T(128)S(6)} %min.3, f32[]{:T(128)} %bitcast), kind=kOutput, calls=%fused_computation.13 | convolution fusion | flops 315801600 | bytes 3522568 | tf_op jit(solution)/shard_map/dot_general | solution.py:60
  259.8 0.0 copy-done.1
  259.8 0.0 copy-start.4
  259.9 0.0 copy-start.5
  259.9 2.9 fusion
  262.8 0.0 all-reduce.2.cloned.1.call-update
  262.8 0.0 copy-done.4
  262.8 0.1 copy.18
  263.0 0.1 copy.22
  263.1 0.1 copy.27
  263.3 0.4 copy-done.7
  263.7 0.1 copy.29
  263.8 0.1 multiply_subtract_fusion
  263.9 0.8 copy.23
  264.8 0.8 copy.24
  265.6 38.5 %all-reduce.2.cloned.1.call-done = f32[64,1280]{1,0:T(8,128)} async-done(((f32[64,1280]{1,0:T(8,128)}), f32[64,1280]{1,0:T(8,128)}) %all-reduce.2.cloned.1.call-update) | async-done | bytes 327696 | tf_op jit(solution)/shard_map/psum | solution.py:61
  304.1 1.7 add_convert_fusion
  (6 shorter events, 0.0 us)
Async XLA Ops:
  7.2 33.3 %all-gather.7.cloned.1.call-start = ((), (), s32[]{:S(2)}) async-start(), calls=%async_computation.2 | async-start | bytes 2211840 | tf_op jit(solution)/shard_map/all_gather | solution.py:27
  7.9 61.7 %all-gather.9.cloned.1.call-start = ((), (), s32[]{:S(2)}) async-start(), calls=%async_computation.3 | async-start | bytes 2211840 | tf_op jit(solution)/shard_map/all_gather | solution.py:28
  8.6 93.8 %all-gather.15.cloned.1.call-start = ((), (), s32[]{:S(2)}) async-start(), calls=%async_computation.7 | async-start | bytes 1638400 | tf_op jit(solution)/shard_map/all_gather | solution.py:8
  43.8 31.1 %copy-start.9 = (f32[2]{0:T(128)S(1)}, f32[2]{0:T(128)}, u32[]{:S(2)}) copy-start(f32[2]{0:T(128)} %param.12) | copy-start | bytes 28
  43.8 32.4 %copy-start.10 = (f32[2,64]{1,0:T(2,128)S(1)}, f32[2,64]{1,0:T(2,128)}, u32[]{:S(2)}) copy-start(f32[2,64]{1,0:T(2,128)} %param.11) | copy-start | bytes 1540
  43.8 60.2 %copy-start.2 = (bf16[2,64,1280]{2,1,0:T(8,128)(2,1)S(1)}, bf16[2,64,1280]{2,1,0:T(8,128)(2,1)}, u32[]{:S(2)}) copy-start(bf16[2,64,1280]{2,1,0:T(8,128)(2,1)} %param.8) | copy-start | bytes 983044
  43.8 60.2 %copy-start.3 = (bf16[2,64,1280]{2,1,0:T(8,128)(2,1)S(1)}, bf16[2,64,1280]{2,1,0:T(8,128)(2,1)}, u32[]{:S(2)}) copy-start(bf16[2,64,1280]{2,1,0:T(8,128)(2,1)} %param.9) | copy-start | bytes 983044
  69.6 34.4 %copy-start = (f32[1280,320]{1,0:T(8,128)S(1)}, f32[1280,320]{1,0:T(8,128)}, u32[]{:S(2)}) copy-start(f32[1280,320]{1,0:T(8,128)} %all-gather.9.cloned.1.call-done) | copy-start | bytes 4915204
  74.2 73.9 %reduce-scatter.7.cloned.1.call-start = ((), (), s32[]{:S(2)}) async-start(), calls=%async_computation.8 | async-start | bytes 2211840 | tf_op jit(solution)/shard_map/reduce_scatter | solution.py:45
  112.1 72.3 %reduce-scatter.9.cloned.1.call-start = ((), (), s32[]{:S(2)}) async-start(), calls=%async_computation.9 | async-start | bytes 2211840 | tf_op jit(solution)/shard_map/reduce_scatter | solution.py:46
  115.9 96.3 %all-gather.11.cloned.1.call-start = ((), (), s32[]{:S(2)}) async-start(), calls=%async_computation.4 | async-start | bytes 2211840 | tf_op jit(solution)/shard_map/all_gather | solution.py:50
  148.1 93.2 %all-gather.13.cloned.1.call-start = ((), (), s32[]{:S(2)}) async-start(), calls=%async_computation.5 | async-start | bytes 2211840 | tf_op jit(solution)/shard_map/all_gather | solution.py:51
  184.4 119.7 %all-reduce.2.cloned.1.call-start = ((), (), s32[]{:S(2)}) async-start(), calls=%async_computation.6 | async-start | bytes 655360 | tf_op jit(solution)/shard_map/psum | solution.py:61
  185.1 71.4 %copy-start.8 = (bf16[64,1280]{1,0:T(8,128)(2,1)S(1)}, bf16[64,1280]{1,0:T(8,128)(2,1)}, u32[]{:S(2)}) copy-start(bf16[64,1280]{1,0:T(8,128)(2,1)} %param.10) | copy-start | bytes 491524
  256.5 3.3 %copy-start.1 = (f32[1280,320]{1,0:T(8,128)S(1)}, f32[1280,320]{1,0:T(8,128)}, u32[]{:S(2)}) copy-start(f32[1280,320]{1,0:T(8,128)} %all-gather.13.cloned.1.call-done) | copy-start | bytes 4915204
  259.8 2.9 copy-start.4
  259.9 3.1 copy-start.5
  259.9 3.2 %copy-start.6 = (f32[160,320]{1,0:T(8,128)S(1)}, f32[160,320]{1,0:T(8,128)}, u32[]{:S(2)}) copy-start(f32[160,320]{1,0:T(8,128)} %reduce-scatter.7.cloned.1.call-done) | copy-start | bytes 614404
  262.8 0.9 copy-start.7
Sparse Core Ops, SparseCore 0:
  9.6 30.7 all-gather.6
  42.1 27.4 all-gather.8
  74.4 28.0 all-gather.14
  112.3 35.7 reduce-scatter.6
  150.3 34.0 reduce-scatter.8
  185.9 26.2 all-gather.10
  213.8 27.4 all-gather.12
  262.9 41.1 all-reduce.1
